TPU v7x, 32 devices: a whole 2x2x4 slice. The times are simulated.
32 devices in a mesh: expert: 8 (over y, x, core), token: 4 (over z).
Axes of the slice: x: 2, y: 2, z: 4, core: 2. Of those that a mesh axis runs over, the one named last changes fastest.
Arguments:
- activations: bfloat16 [16, 1024, 768], P('expert', 'token'), may hold values from -6 to 6
- routed: int32 [16, 1024], P('expert', 'token'), may hold values 0 or 1
- weights: bfloat16 [128, 768, 256], P(('expert', 'token')), may hold values from -6 to 6, as said below
- kept_mask: int32 [128, 768, 256], P(('expert', 'token')), may hold values 0 or 1
- step_counts: int32 [128], P(('expert', 'token')), may hold values from 1 to 7
- ridge_scale: float32 [128], P(('expert', 'token')), may hold values from 0.05 to 0.5
Outputs:
- rebuilt: float32 [128, 768, 256], P(('expert', 'token'))
- misfit: float32 [16], P('expert')
Inputs may be any that keep to these rules, and one draw needn't show every extreme that they name: `weights`: every entry's magnitude is at least 0.25.
All inputs are finite; a program needn't handle non-finite values. No bound on the sum of `routed` or of `kept_mask` on one device may be relied on, other than what follows from the above.
Results may differ from a plain program's by a relative error of at most 0.0003.
Values may be sent and summed in bfloat16 or wider, within the bound.
A program may use at most 64 MiB of HBM per device.

v0:
```python
import jax
import jax.numpy as jnp
from jax import lax
from jax.sharding import PartitionSpec as P

D = 2048
COLS = 256


def solve_task(gram_matrix, frobenius, task_weights, task_mask, task_count, task_ridge):
    float_weights = task_weights.astype(jnp.float32)
    float_mask = task_mask.astype(jnp.float32)
    damping = task_ridge * frobenius
    step_size = 1.0 / (frobenius + damping)

    def advance(turn_index, current):
        gradient = (
            jnp.dot(gram_matrix, current - float_weights, precision=lax.Precision.HIGHEST)
            + damping * current
        )
        return current - step_size * (float_mask * gradient)

    result = lax.fori_loop(0, task_count, advance, float_mask * float_weights)
    change = result - float_weights
    numerator = jnp.sum(change * jnp.dot(gram_matrix, change, precision=lax.Precision.HIGHEST))
    energy = jnp.sum(
        float_weights * jnp.dot(gram_matrix, float_weights, precision=lax.Precision.HIGHEST)
    )
    return (result, numerator, energy)


def on_device(activations, routed, weights, kept_mask, step_counts, ridge_scale):
    local_experts, row_count, features = activations.shape
    local_tasks = weights.shape[0]
    per_expert = D // COLS
    total_rows = row_count * lax.axis_size("token")
    own_slot = lax.axis_index("token") * local_tasks // per_expert
    masked = activations * routed[:, :, None].astype(jnp.bfloat16)
    own_rows = lax.dynamic_index_in_dim(
        lax.all_gather(masked, "token", axis=1, tiled=True), own_slot, 0, keepdims=False
    )
    gram_sum = lax.dot_general(
        own_rows, own_rows, (((0,), (0,)), ((), ())), preferred_element_type=jnp.float32
    )
    gram_matrix = gram_sum / total_rows
    frobenius = jnp.sqrt(jnp.sum(gram_matrix * gram_matrix))

    def one_task(task_args):
        task_weights, task_mask, task_count, task_ridge = task_args
        return solve_task(gram_matrix, frobenius, task_weights, task_mask, task_count, task_ridge)

    rebuilt, numerators, energies = lax.map(
        one_task, (weights, kept_mask, step_counts, ridge_scale)
    )
    picker = (jnp.arange(local_experts) == own_slot).astype(jnp.float32)
    expert_terms = lax.psum(picker * jnp.sum(numerators), "token")
    layer_energy = lax.psum(jnp.sum(energies), ("expert", "token"))
    expert_total = local_experts * lax.axis_size("expert")
    misfit = expert_terms / (layer_energy / expert_total + 1e-06)
    return (rebuilt, misfit)


def solution(mesh):
    placed = (
        P("expert", "token", None),
        P("expert", "token"),
        P(("expert", "token"), None, None),
        P(("expert", "token"), None, None),
        P(("expert", "token")),
        P(("expert", "token")),
    )
    return jax.shard_map(
        on_device,
        mesh=mesh,
        in_specs=placed,
        out_specs=(P(("expert", "token"), None, None), P("expert")),
        check_vma=False,
    )
```

profile of v0, /device:TPU:0, one launch (start us, length us, event | category | flops | bytes accessed | tf_op | source)
XLA Modules:
  0.0 320.7 jit_solution(10718532296523301616)
XLA Ops:
  10.2 66.2 %all-gather.2.cloned.1.call-done = bf16[2,1024,768]{2,1,0:T(8,128)(2,1)} async-done(((bf16[2,256,768]{2,1,0:T(8,128)(2,1)}), bf16[2,1024,768]{2,1,0:T(8,128)(2,1)}) %all-gather.2.cloned.1.call-update) | async-done | bytes 3145744 | tf_op jit(solution)/shard_map/all_gather | solution.py:40
  76.4 4.1 %multiply_reduce_fusion = (f32[]{:T(128)}, f32[768,768]{1,0:T(8,128)S(1)}) fusion(bf16[2,1024,768]{2,1,0:T(8,128)(2,1)} %all-gather.2.cloned.1.call-done, s32[]{:T(128)S(6)} %select_n.10), kind=kOutput, calls=%fused_computation.22 | convolution fusion | flops 1209729024 | bytes 3932168 | tf_op jit(solution)/shard_map/dot_general | solution.py:42
  81.1 163.0 %while.25 = (s32[]{:T(128)}, f32[4,768,256]{2,1,0:T(8,128)}, f32[4]{0:T(128)S(1)}, f32[4]{0:T(128)S(1)}, s32[4,768,256]{2,1,0:T(8,128)}, /*index=5*/bf16[4,768,2...) while((s32[]{:T(128)}, f32[4,768,256]{2,1,0:T(8,128)}, ...), condition=%wide.region_6.7_spmd, body=%wide.region_1.6_spmd.sunk | while | flops 5439750144 | bytes 29491652 | solution.py:52
  84.1 2.2 fusion.35
  94.6 27.0 %while.26 = (s32[]{:T(128)}, f32[768,256]{0,1:T(8,128)S(1)}, s32[]{:T(128)}, f32[]{:T(128)}, f32[768,256]{0,1:T(8,128)}, /*index=5*/f32[768,768]{1,0:T(8,128)S(1)}, f32[]{:T(128)}, f32[768,256]{0,1:T(8,128)}, s32[]{:T(128)}) while((s32[]{:T(128)}, f32[768,256]{0,1:T(8,128)S(1)}, s32[]{:T(128)}, f32[]{:T(128)}, f32[768,256]{0,1:T(8,128)}, ...), condition=%wide.region_3.3_spmd, body=%wide.region_2.2_spmd.sunk | while | flops 1813118976 | bytes 7077989 | solution.py:23
  95.3 3.7 %fusion.38 = f32[768,256]{0,1:T(8,128)S(1)} fusion(f32[768,256]{0,1:T(8,128)S(1)} %copy.48, f32[768,256]{0,1:T(8,128)} %get-tuple-element.307, f32[768,768]{1,0:T(8,128)S(1)} %get-tuple-element.305, f32[768,256]{0,1:T(8,128)} %get-tuple-element.304, f32[]{:T(128)} %get-tuple-element.306, f32[]{:T(128)} %get-tuple-element.303), kind=kOutput, calls=%fused_computation.4.clone.1 | convolution fusion | flops 1813118976 | bytes 5505032 | tf_op jit(solution)/shard_map/while/body/eval_jaxpr/while/body/dot_general | solution.py:18
  99.7 3.7 %fusion.38 = f32[768,256]{0,1:T(8,128)S(1)} fusion(f32[768,256]{0,1:T(8,128)S(1)} %copy.48, f32[768,256]{0,1:T(8,128)} %get-tuple-element.307, f32[768,768]{1,0:T(8,128)S(1)} %get-tuple-element.305, f32[768,256]{0,1:T(8,128)} %get-tuple-element.304, f32[]{:T(128)} %get-tuple-element.306, f32[]{:T(128)} %get-tuple-element.303), kind=kOutput, calls=%fused_computation.4.clone.1 | convolution fusion | flops 1813118976 | bytes 5505032 | tf_op jit(solution)/shard_map/while/body/eval_jaxpr/while/body/dot_general | solution.py:18
  104.1 3.7 %fusion.38 = f32[768,256]{0,1:T(8,128)S(1)} fusion(f32[768,256]{0,1:T(8,128)S(1)} %copy.48, f32[768,256]{0,1:T(8,128)} %get-tuple-element.307, f32[768,768]{1,0:T(8,128)S(1)} %get-tuple-element.305, f32[768,256]{0,1:T(8,128)} %get-tuple-element.304, f32[]{:T(128)} %get-tuple-element.306, f32[]{:T(128)} %get-tuple-element.303), kind=kOutput, calls=%fused_computation.4.clone.1 | convolution fusion | flops 1813118976 | bytes 5505032 | tf_op jit(solution)/shard_map/while/body/eval_jaxpr/while/body/dot_general | solution.py:18
  108.5 3.7 %fusion.38 = f32[768,256]{0,1:T(8,128)S(1)} fusion(f32[768,256]{0,1:T(8,128)S(1)} %copy.48, f32[768,256]{0,1:T(8,128)} %get-tuple-element.307, f32[768,768]{1,0:T(8,128)S(1)} %get-tuple-element.305, f32[768,256]{0,1:T(8,128)} %get-tuple-element.304, f32[]{:T(128)} %get-tuple-element.306, f32[]{:T(128)} %get-tuple-element.303), kind=kOutput, calls=%fused_computation.4.clone.1 | convolution fusion | flops 1813118976 | bytes 5505032 | tf_op jit(solution)/shard_map/while/body/eval_jaxpr/while/body/dot_general | solution.py:18
  112.9 3.7 %fusion.38 = f32[768,256]{0,1:T(8,128)S(1)} fusion(f32[768,256]{0,1:T(8,128)S(1)} %copy.48, f32[768,256]{0,1:T(8,128)} %get-tuple-element.307, f32[768,768]{1,0:T(8,128)S(1)} %get-tuple-element.305, f32[768,256]{0,1:T(8,128)} %get-tuple-element.304, f32[]{:T(128)} %get-tuple-element.306, f32[]{:T(128)} %get-tuple-element.303), kind=kOutput, calls=%fused_computation.4.clone.1 | convolution fusion | flops 1813118976 | bytes 5505032 | tf_op jit(solution)/shard_map/while/body/eval_jaxpr/while/body/dot_general | solution.py:18
  117.3 3.7 %fusion.38 = f32[768,256]{0,1:T(8,128)S(1)} fusion(f32[768,256]{0,1:T(8,128)S(1)} %copy.48, f32[768,256]{0,1:T(8,128)} %get-tuple-element.307, f32[768,768]{1,0:T(8,128)S(1)} %get-tuple-element.305, f32[768,256]{0,1:T(8,128)} %get-tuple-element.304, f32[]{:T(128)} %get-tuple-element.306, f32[]{:T(128)} %get-tuple-element.303), kind=kOutput, calls=%fused_computation.4.clone.1 | convolution fusion | flops 1813118976 | bytes 5505032 | tf_op jit(solution)/shard_map/while/body/eval_jaxpr/while/body/dot_general | solution.py:18
  121.6 2.9 fusion.34
  142.0 27.0 %while.26 = (s32[]{:T(128)}, f32[768,256]{0,1:T(8,128)S(1)}, s32[]{:T(128)}, f32[]{:T(128)}, f32[768,256]{0,1:T(8,128)}, /*index=5*/f32[768,768]{1,0:T(8,128)S(1)}, f32[]{:T(128)}, f32[768,256]{0,1:T(8,128)}, s32[]{:T(128)}) while((s32[]{:T(128)}, f32[768,256]{0,1:T(8,128)S(1)}, s32[]{:T(128)}, f32[]{:T(128)}, f32[768,256]{0,1:T(8,128)}, ...), condition=%wide.region_3.3_spmd, body=%wide.region_2.2_spmd.sunk | while | flops 1813118976 | bytes 7077989 | solution.py:23
  142.7 3.7 %fusion.38 = f32[768,256]{0,1:T(8,128)S(1)} fusion(f32[768,256]{0,1:T(8,128)S(1)} %copy.48, f32[768,256]{0,1:T(8,128)} %get-tuple-element.307, f32[768,768]{1,0:T(8,128)S(1)} %get-tuple-element.305, f32[768,256]{0,1:T(8,128)} %get-tuple-element.304, f32[]{:T(128)} %get-tuple-element.306, f32[]{:T(128)} %get-tuple-element.303), kind=kOutput, calls=%fused_computation.4.clone.1 | convolution fusion | flops 1813118976 | bytes 5505032 | tf_op jit(solution)/shard_map/while/body/eval_jaxpr/while/body/dot_general | solution.py:18
  147.1 3.7 %fusion.38 = f32[768,256]{0,1:T(8,128)S(1)} fusion(f32[768,256]{0,1:T(8,128)S(1)} %copy.48, f32[768,256]{0,1:T(8,128)} %get-tuple-element.307, f32[768,768]{1,0:T(8,128)S(1)} %get-tuple-element.305, f32[768,256]{0,1:T(8,128)} %get-tuple-element.304, f32[]{:T(128)} %get-tuple-element.306, f32[]{:T(128)} %get-tuple-element.303), kind=kOutput, calls=%fused_computation.4.clone.1 | convolution fusion | flops 1813118976 | bytes 5505032 | tf_op jit(solution)/shard_map/while/body/eval_jaxpr/while/body/dot_general | solution.py:18
  151.5 3.7 %fusion.38 = f32[768,256]{0,1:T(8,128)S(1)} fusion(f32[768,256]{0,1:T(8,128)S(1)} %copy.48, f32[768,256]{0,1:T(8,128)} %get-tuple-element.307, f32[768,768]{1,0:T(8,128)S(1)} %get-tuple-element.305, f32[768,256]{0,1:T(8,128)} %get-tuple-element.304, f32[]{:T(128)} %get-tuple-element.306, f32[]{:T(128)} %get-tuple-element.303), kind=kOutput, calls=%fused_computation.4.clone.1 | convolution fusion | flops 1813118976 | bytes 5505032 | tf_op jit(solution)/shard_map/while/body/eval_jaxpr/while/body/dot_general | solution.py:18
  155.8 3.7 %fusion.38 = f32[768,256]{0,1:T(8,128)S(1)} fusion(f32[768,256]{0,1:T(8,128)S(1)} %copy.48, f32[768,256]{0,1:T(8,128)} %get-tuple-element.307, f32[768,768]{1,0:T(8,128)S(1)} %get-tuple-element.305, f32[768,256]{0,1:T(8,128)} %get-tuple-element.304, f32[]{:T(128)} %get-tuple-element.306, f32[]{:T(128)} %get-tuple-element.303), kind=kOutput, calls=%fused_computation.4.clone.1 | convolution fusion | flops 1813118976 | bytes 5505032 | tf_op jit(solution)/shard_map/while/body/eval_jaxpr/while/body/dot_general | solution.py:18
  160.2 3.7 %fusion.38 = f32[768,256]{0,1:T(8,128)S(1)} fusion(f32[768,256]{0,1:T(8,128)S(1)} %copy.48, f32[768,256]{0,1:T(8,128)} %get-tuple-element.307, f32[768,768]{1,0:T(8,128)S(1)} %get-tuple-element.305, f32[768,256]{0,1:T(8,128)} %get-tuple-element.304, f32[]{:T(128)} %get-tuple-element.306, f32[]{:T(128)} %get-tuple-element.303), kind=kOutput, calls=%fused_computation.4.clone.1 | convolution fusion | flops 1813118976 | bytes 5505032 | tf_op jit(solution)/shard_map/while/body/eval_jaxpr/while/body/dot_general | solution.py:18
  164.6 3.7 %fusion.38 = f32[768,256]{0,1:T(8,128)S(1)} fusion(f32[768,256]{0,1:T(8,128)S(1)} %copy.48, f32[768,256]{0,1:T(8,128)} %get-tuple-element.307, f32[768,768]{1,0:T(8,128)S(1)} %get-tuple-element.305, f32[768,256]{0,1:T(8,128)} %get-tuple-element.304, f32[]{:T(128)} %get-tuple-element.306, f32[]{:T(128)} %get-tuple-element.303), kind=kOutput, calls=%fused_computation.4.clone.1 | convolution fusion | flops 1813118976 | bytes 5505032 | tf_op jit(solution)/shard_map/while/body/eval_jaxpr/while/body/dot_general | solution.py:18
  168.9 2.9 fusion.34
  189.3 13.8 %while.26 = (s32[]{:T(128)}, f32[768,256]{0,1:T(8,128)S(1)}, s32[]{:T(128)}, f32[]{:T(128)}, f32[768,256]{0,1:T(8,128)}, /*index=5*/f32[768,768]{1,0:T(8,128)S(1)}, f32[]{:T(128)}, f32[768,256]{0,1:T(8,128)}, s32[]{:T(128)}) while((s32[]{:T(128)}, f32[768,256]{0,1:T(8,128)S(1)}, s32[]{:T(128)}, f32[]{:T(128)}, f32[768,256]{0,1:T(8,128)}, ...), condition=%wide.region_3.3_spmd, body=%wide.region_2.2_spmd.sunk | while | flops 1813118976 | bytes 7077989 | solution.py:23
  190.0 3.7 %fusion.38 = f32[768,256]{0,1:T(8,128)S(1)} fusion(f32[768,256]{0,1:T(8,128)S(1)} %copy.48, f32[768,256]{0,1:T(8,128)} %get-tuple-element.307, f32[768,768]{1,0:T(8,128)S(1)} %get-tuple-element.305, f32[768,256]{0,1:T(8,128)} %get-tuple-element.304, f32[]{:T(128)} %get-tuple-element.306, f32[]{:T(128)} %get-tuple-element.303), kind=kOutput, calls=%fused_computation.4.clone.1 | convolution fusion | flops 1813118976 | bytes 5505032 | tf_op jit(solution)/shard_map/while/body/eval_jaxpr/while/body/dot_general | solution.py:18
  194.4 3.7 %fusion.38 = f32[768,256]{0,1:T(8,128)S(1)} fusion(f32[768,256]{0,1:T(8,128)S(1)} %copy.48, f32[768,256]{0,1:T(8,128)} %get-tuple-element.307, f32[768,768]{1,0:T(8,128)S(1)} %get-tuple-element.305, f32[768,256]{0,1:T(8,128)} %get-tuple-element.304, f32[]{:T(128)} %get-tuple-element.306, f32[]{:T(128)} %get-tuple-element.303), kind=kOutput, calls=%fused_computation.4.clone.1 | convolution fusion | flops 1813118976 | bytes 5505032 | tf_op jit(solution)/shard_map/while/body/eval_jaxpr/while/body/dot_general | solution.py:18
  198.8 3.7 %fusion.38 = f32[768,256]{0,1:T(8,128)S(1)} fusion(f32[768,256]{0,1:T(8,128)S(1)} %copy.48, f32[768,256]{0,1:T(8,128)} %get-tuple-element.307, f32[768,768]{1,0:T(8,128)S(1)} %get-tuple-element.305, f32[768,256]{0,1:T(8,128)} %get-tuple-element.304, f32[]{:T(128)} %get-tuple-element.306, f32[]{:T(128)} %get-tuple-element.303), kind=kOutput, calls=%fused_computation.4.clone.1 | convolution fusion | flops 1813118976 | bytes 5505032 | tf_op jit(solution)/shard_map/while/body/eval_jaxpr/while/body/dot_general | solution.py:18
  203.1 2.9 fusion.34
  223.5 13.8 %while.26 = (s32[]{:T(128)}, f32[768,256]{0,1:T(8,128)S(1)}, s32[]{:T(128)}, f32[]{:T(128)}, f32[768,256]{0,1:T(8,128)}, /*index=5*/f32[768,768]{1,0:T(8,128)S(1)}, f32[]{:T(128)}, f32[768,256]{0,1:T(8,128)}, s32[]{:T(128)}) while((s32[]{:T(128)}, f32[768,256]{0,1:T(8,128)S(1)}, s32[]{:T(128)}, f32[]{:T(128)}, f32[768,256]{0,1:T(8,128)}, ...), condition=%wide.region_3.3_spmd, body=%wide.region_2.2_spmd.sunk | while | flops 1813118976 | bytes 7077989 | solution.py:23
  224.2 3.7 %fusion.38 = f32[768,256]{0,1:T(8,128)S(1)} fusion(f32[768,256]{0,1:T(8,128)S(1)} %copy.48, f32[768,256]{0,1:T(8,128)} %get-tuple-element.307, f32[768,768]{1,0:T(8,128)S(1)} %get-tuple-element.305, f32[768,256]{0,1:T(8,128)} %get-tuple-element.304, f32[]{:T(128)} %get-tuple-element.306, f32[]{:T(128)} %get-tuple-element.303), kind=kOutput, calls=%fused_computation.4.clone.1 | convolution fusion | flops 1813118976 | bytes 5505032 | tf_op jit(solution)/shard_map/while/body/eval_jaxpr/while/body/dot_general | solution.py:18
  228.6 3.7 %fusion.38 = f32[768,256]{0,1:T(8,128)S(1)} fusion(f32[768,256]{0,1:T(8,128)S(1)} %copy.48, f32[768,256]{0,1:T(8,128)} %get-tuple-element.307, f32[768,768]{1,0:T(8,128)S(1)} %get-tuple-element.305, f32[768,256]{0,1:T(8,128)} %get-tuple-element.304, f32[]{:T(128)} %get-tuple-element.306, f32[]{:T(128)} %get-tuple-element.303), kind=kOutput, calls=%fused_computation.4.clone.1 | convolution fusion | flops 1813118976 | bytes 5505032 | tf_op jit(solution)/shard_map/while/body/eval_jaxpr/while/body/dot_general | solution.py:18
  233.0 3.7 %fusion.38 = f32[768,256]{0,1:T(8,128)S(1)} fusion(f32[768,256]{0,1:T(8,128)S(1)} %copy.48, f32[768,256]{0,1:T(8,128)} %get-tuple-element.307, f32[768,768]{1,0:T(8,128)S(1)} %get-tuple-element.305, f32[768,256]{0,1:T(8,128)} %get-tuple-element.304, f32[]{:T(128)} %get-tuple-element.306, f32[]{:T(128)} %get-tuple-element.303), kind=kOutput, calls=%fused_computation.4.clone.1 | convolution fusion | flops 1813118976 | bytes 5505032 | tf_op jit(solution)/shard_map/while/body/eval_jaxpr/while/body/dot_general | solution.py:18
  237.3 2.9 fusion.34
  246.0 11.4 %psum.14 = f32[2]{0:T(128)S(1)} all-reduce(f32[2]{0:T(128)S(1)} %compare_select_fusion), channel_id=1, replica_groups=mesh['expert'=8,'token'=4] {'token'}, use_global_device_ids=true, to_apply=%region_8.9 | all-reduce | flops 2 | bytes 16 | tf_op jit(solution)/shard_map/psum | solution.py:56
  257.4 55.3 %psum.15 = f32[]{:T(128)} all-reduce(f32[]{:T(128)} %reduce_sum.47), channel_id=1, replica_groups=mesh['expert'=8,'token'=4] {'expert','token'}, use_global_device_ids=true, to_apply=%region_10.11 | all-reduce | flops 1 | bytes 8 | tf_op jit(solution)/shard_map/psum | solution.py:57
  (96 shorter events, 71.4 us)
Async XLA Ops:
  7.2 69.2 %all-gather.2.cloned.1.call-start = ((), (), s32[]{:S(2)}) async-start(), calls=%async_computation | async-start | bytes 3932160 | tf_op jit(solution)/shard_map/all_gather | solution.py:40
  10.1 71.0 %copy-start.1 = (s32[4]{0:T(128)S(1)}, s32[4]{0:T(128)}, u32[]{:S(2)}) copy-start(s32[4]{0:T(128)} %param.14) | copy-start | bytes 52
  10.1 71.0 %copy-start.2 = (f32[4]{0:T(128)S(1)}, f32[4]{0:T(128)}, u32[]{:S(2)}) copy-start(f32[4]{0:T(128)} %param.15) | copy-start | bytes 52
  91.6 0.9 copy-start
  138.9 0.9 copy-start
  186.3 0.9 copy-start
  220.4 0.9 copy-start
Sparse Core Ops, SparseCore 0:
  10.2 66.1 all-gather.1
where the time goes:
time: 323 us; the launch traced here: 321 us
  matrix products  90.8 us (28%)
  blocking collectives  66.7 us (21%)
  waiting for transfers between devices  66.3 us (21%)
  local copies, waits for them, and re-layouts  47.1 us (15%)
  other arithmetic  17.6 us (5%)
  loops' own time  16.9 us (5%)
  between operations  15.4 us (5%)
    dot_general x18, matrix products, advance(): jnp.dot(gram_matrix, current - float_weights, precision=lax.Precision.HIG...  66.3 us
    all_gather x1, waiting for transfers between devices, on_device(): lax.all_gather(masked, 'token', axis=1, tiled=True)  66.2 us
    psum x1, blocking collectives, on_device(): layer_energy = lax.psum(jnp.sum(energies), ('expert', 'token'))  55.3 us
    dynamic_slice x24, local copies, waits for them, and re-layouts, on_device(): lax.map(one_task, (weights, kept_mask, step_counts, ridge_scale))  23.4 us
    dynamic_update_slice x16, local copies, waits for them, and re-layouts, on_device(): lax.map(one_task, (weights, kept_mask, step_counts, ridge_scale))  19.2 us
    another operation x4, loops' own time, solve_task(): result = lax.fori_loop(0, task_count, advance, float_mask * float_weights)  14.3 us
    dot_general x4, matrix products, solve_task(): jnp.dot(gram_matrix, change, precision=lax.Precision.HIGHEST)  11.5 us
    psum x1, blocking collectives, on_device(): expert_terms = lax.psum(picker * jnp.sum(numerators), 'token')  11.4 us
  transfers between devices with their start and end apart: 1, of which 1 were waited for; matrix products, arithmetic and copies ran while one was open for 0% of the time, Pallas kernels for 0%

commit v1 on v0

--- a/solution.py
+++ b/solution.py
@@ -30,15 +30,34 @@
 
 
 def on_device(activations, routed, weights, kept_mask, step_counts, ridge_scale):
+
+    def patch_raise(incoming_x, lane_axis):
+        front, view_out, right_arr = (
+            lax.psum(1, axis_name=lane_axis),
+            lax.axis_index(lane_axis),
+            incoming_x.shape[1],
+        )
+        heap = [(hop_no, (hop_no + 1) % front) for hop_no in range(front)]
+        high = jnp.zeros(
+            (*incoming_x.shape[:1], front * right_arr, *incoming_x.shape[2:]), incoming_x.dtype
+        )
+        response = incoming_x
+        it = 0
+        while it < front:
+            w_next = (view_out - it) % front
+            high = lax.dynamic_update_slice_in_dim(high, response, w_next * right_arr, axis=1)
+            if it < front - 1:
+                response = lax.ppermute(response, lane_axis, heap)
+            it += 1
+        return high
+
     local_experts, row_count, features = activations.shape
     local_tasks = weights.shape[0]
     per_expert = D // COLS
     total_rows = row_count * lax.axis_size("token")
     own_slot = lax.axis_index("token") * local_tasks // per_expert
     masked = activations * routed[:, :, None].astype(jnp.bfloat16)
-    own_rows = lax.dynamic_index_in_dim(
-        lax.all_gather(masked, "token", axis=1, tiled=True), own_slot, 0, keepdims=False
-    )
+    own_rows = lax.dynamic_index_in_dim(patch_raise(masked, "token"), own_slot, 0, keepdims=False)
     gram_sum = lax.dot_general(
         own_rows, own_rows, (((0,), (0,)), ((), ())), preferred_element_type=jnp.float32
     )

time: 323 us -> 307 us (0.950)
  between operations: 15.4 us -> 1.93 us
  waiting for transfers between devices: 66.3 us -> 57.8 us
  local copies, waits for them, and re-layouts: 47.1 us -> 51.9 us
    all_gather x1 -> x0, waiting for transfers between devices: 66.2 us -> none  [on_device(): lax.all_gather(masked, 'token', axis=1, tiled=True)]
    ppermute x0 -> x3, waiting for transfers between devices: none -> 57.8 us  [patch_raise(): response = lax.ppermute(response, lane_axis, heap)]
  transfers between devices with their start and end apart: 1 -> 3, of which waited for: 1 -> 3; matrix products, arithmetic and copies ran while one was open for 0% -> 1% of each run, Pallas kernels for 0% -> 0%
where the time goes in v1:
time: 307 us; the launch traced here: 305 us
  matrix products  90.8 us (30%)
  blocking collectives  66.4 us (22%)
  waiting for transfers between devices  57.8 us (19%)
  local copies, waits for them, and re-layouts  51.9 us (17%)
  loops' own time  16.9 us (6%)
  other arithmetic  16.6 us (5%)
  starting transfers between devices  3.08 us (1%)
    dot_general x18, matrix products, advance(): jnp.dot(gram_matrix, current - float_weights, precision=lax.Precision.HIG...  66.3 us
    psum x1, blocking collectives, on_device(): layer_energy = lax.psum(jnp.sum(energies), ('expert', 'token'))  58.1 us
    ppermute x3, waiting for transfers between devices, patch_raise(): response = lax.ppermute(response, lane_axis, heap)  57.8 us
    dynamic_slice x24, local copies, waits for them, and re-layouts, on_device(): lax.map(one_task, (weights, kept_mask, step_counts, ridge_scale))  23.4 us
    dynamic_update_slice x16, local copies, waits for them, and re-layouts, on_device(): lax.map(one_task, (weights, kept_mask, step_counts, ridge_scale))  19.2 us
    another operation x4, loops' own time, solve_task(): result = lax.fori_loop(0, task_count, advance, float_mask * float_weights)  14.3 us
    dot_general x4, matrix products, solve_task(): jnp.dot(gram_matrix, change, precision=lax.Precision.HIGHEST)  11.5 us
    dot_general x4, matrix products, solve_task(): jnp.dot(gram_matrix, float_weights, precision=lax.Precision.HIGHEST)  8.88 us
  transfers between devices with their start and end apart: 3, of which 3 were waited for; matrix products, arithmetic and copies ran while one was open for 1% of the time, Pallas kernels for 0%

profile of v1, /device:TPU:0, one launch (start us, length us, event | category | flops | bytes accessed | tf_op | source)
XLA Modules:
  0.0 305.4 jit_solution(2503206601856717499)
XLA Ops:
  4.3 3.1 %collective-permute-start = (bf16[2,256,768]{2,1,0:T(8,128)(2,1)S(1)}, bf16[2,256,768]{2,1,0:T(8,128)(2,1)S(1)}, u32[]{:S(2)}, u32[]{:S(2)}) collective-permute-start(bf16[2,256,768]{2,1,0:T(8,128)(2,1)S(1)} %get-tuple-element.151), channel_id=1, source_target_pairs={{0,1},{1,2},{2,3},{3,0},{4,5},{5,6},{6,7},{7,4},{8,9},{9,10},{10,1... | collective-permute-start | bytes 2359304 | tf_op jit(solution)/shard_map/ppermute | solution.py:50
  7.4 19.6 %collective-permute-done = bf16[2,256,768]{2,1,0:T(8,128)(2,1)S(1)} collective-permute-done((bf16[2,256,768]{2,1,0:T(8,128)(2,1)S(1)}, bf16[2,256,768]{2,1,0:T(8,128)(2,1)S(1)}, u32[]{:S(2)}, u32[]{:S(2)}) %collective-permute-start) | collective-permute-done | bytes 786464 | tf_op jit(solution)/shard_map/ppermute | solution.py:50
  27.0 20.5 %collective-permute-done.1 = bf16[2,256,768]{2,1,0:T(8,128)(2,1)S(1)} collective-permute-done((bf16[2,256,768]{2,1,0:T(8,128)(2,1)S(1)}, bf16[2,256,768]{2,1,0:T(8,128)(2,1)S(1)}, u32[]{:S(2)}, u32[]{:S(2)}) %collective-permute-start.1) | collective-permute-done | bytes 786464 | tf_op jit(solution)/shard_map/ppermute | solution.py:50
  49.5 17.7 %collective-permute-done.2 = bf16[2,256,768]{2,1,0:T(8,128)(2,1)S(1)} collective-permute-done((bf16[2,256,768]{2,1,0:T(8,128)(2,1)S(1)}, bf16[2,256,768]{2,1,0:T(8,128)(2,1)S(1)}, u32[]{:S(2)}, u32[]{:S(2)}) %collective-permute-start.2) | collective-permute-done | bytes 786464 | tf_op jit(solution)/shard_map/ppermute | solution.py:50
  68.1 4.1 %multiply_reduce_fusion = (f32[]{:T(128)}, f32[768,768]{1,0:T(8,128)S(1)}) fusion(bf16[2,1024,768]{2,1,0:T(8,128)(2,1)} %constant_dynamic-update-slice_fusion.1, s32[]{:T(128)S(6)} %select_n.48), kind=kOutput, calls=%fused_computation.22 | convolution fusion | flops 1209729024 | bytes 3932168 | tf_op jit(solution)/shard_map/dot_general | solution.py:61
  72.9 163.0 %while.25 = (s32[]{:T(128)}, f32[4,768,256]{2,1,0:T(8,128)}, f32[4]{0:T(128)S(1)}, f32[4]{0:T(128)S(1)}, s32[4,768,256]{2,1,0:T(8,128)}, /*index=5*/bf16[4,768,2...) while((s32[]{:T(128)}, f32[4,768,256]{2,1,0:T(8,128)}, ...), condition=%wide.region_6.7_spmd, body=%wide.region_1.6_spmd.sunk | while | flops 5439750144 | bytes 29491652 | solution.py:71
  86.4 27.0 %while.26 = (s32[]{:T(128)}, f32[768,256]{0,1:T(8,128)S(1)}, s32[]{:T(128)}, f32[]{:T(128)}, f32[768,256]{0,1:T(8,128)}, /*index=5*/f32[768,768]{1,0:T(8,128)S(1)}, f32[]{:T(128)}, f32[768,256]{0,1:T(8,128)}, s32[]{:T(128)}) while((s32[]{:T(128)}, f32[768,256]{0,1:T(8,128)S(1)}, s32[]{:T(128)}, f32[]{:T(128)}, f32[768,256]{0,1:T(8,128)}, ...), condition=%wide.region_3.3_spmd, body=%wide.region_2.2_spmd.sunk | while | flops 1813118976 | bytes 7077989 | solution.py:23
  87.1 3.7 %fusion.38 = f32[768,256]{0,1:T(8,128)S(1)} fusion(f32[768,256]{0,1:T(8,128)S(1)} %copy.52, f32[768,256]{0,1:T(8,128)} %get-tuple-element.309, f32[768,768]{1,0:T(8,128)S(1)} %get-tuple-element.307, f32[768,256]{0,1:T(8,128)} %get-tuple-element.306, f32[]{:T(128)} %get-tuple-element.308, f32[]{:T(128)} %get-tuple-element.305), kind=kOutput, calls=%fused_computation.4.clone.1 | convolution fusion | flops 1813118976 | bytes 5505032 | tf_op jit(solution)/shard_map/while/body/eval_jaxpr/while/body/dot_general | solution.py:18
  91.5 3.7 %fusion.38 = f32[768,256]{0,1:T(8,128)S(1)} fusion(f32[768,256]{0,1:T(8,128)S(1)} %copy.52, f32[768,256]{0,1:T(8,128)} %get-tuple-element.309, f32[768,768]{1,0:T(8,128)S(1)} %get-tuple-element.307, f32[768,256]{0,1:T(8,128)} %get-tuple-element.306, f32[]{:T(128)} %get-tuple-element.308, f32[]{:T(128)} %get-tuple-element.305), kind=kOutput, calls=%fused_computation.4.clone.1 | convolution fusion | flops 1813118976 | bytes 5505032 | tf_op jit(solution)/shard_map/while/body/eval_jaxpr/while/body/dot_general | solution.py:18
  95.8 3.7 %fusion.38 = f32[768,256]{0,1:T(8,128)S(1)} fusion(f32[768,256]{0,1:T(8,128)S(1)} %copy.52, f32[768,256]{0,1:T(8,128)} %get-tuple-element.309, f32[768,768]{1,0:T(8,128)S(1)} %get-tuple-element.307, f32[768,256]{0,1:T(8,128)} %get-tuple-element.306, f32[]{:T(128)} %get-tuple-element.308, f32[]{:T(128)} %get-tuple-element.305), kind=kOutput, calls=%fused_computation.4.clone.1 | convolution fusion | flops 1813118976 | bytes 5505032 | tf_op jit(solution)/shard_map/while/body/eval_jaxpr/while/body/dot_general | solution.py:18
  100.2 3.7 %fusion.38 = f32[768,256]{0,1:T(8,128)S(1)} fusion(f32[768,256]{0,1:T(8,128)S(1)} %copy.52, f32[768,256]{0,1:T(8,128)} %get-tuple-element.309, f32[768,768]{1,0:T(8,128)S(1)} %get-tuple-element.307, f32[768,256]{0,1:T(8,128)} %get-tuple-element.306, f32[]{:T(128)} %get-tuple-element.308, f32[]{:T(128)} %get-tuple-element.305), kind=kOutput, calls=%fused_computation.4.clone.1 | convolution fusion | flops 1813118976 | bytes 5505032 | tf_op jit(solution)/shard_map/while/body/eval_jaxpr/while/body/dot_general | solution.py:18
  104.6 3.7 %fusion.38 = f32[768,256]{0,1:T(8,128)S(1)} fusion(f32[768,256]{0,1:T(8,128)S(1)} %copy.52, f32[768,256]{0,1:T(8,128)} %get-tuple-element.309, f32[768,768]{1,0:T(8,128)S(1)} %get-tuple-element.307, f32[768,256]{0,1:T(8,128)} %get-tuple-element.306, f32[]{:T(128)} %get-tuple-element.308, f32[]{:T(128)} %get-tuple-element.305), kind=kOutput, calls=%fused_computation.4.clone.1 | convolution fusion | flops 1813118976 | bytes 5505032 | tf_op jit(solution)/shard_map/while/body/eval_jaxpr/while/body/dot_general | solution.py:18
  109.0 3.7 %fusion.38 = f32[768,256]{0,1:T(8,128)S(1)} fusion(f32[768,256]{0,1:T(8,128)S(1)} %copy.52, f32[768,256]{0,1:T(8,128)} %get-tuple-element.309, f32[768,768]{1,0:T(8,128)S(1)} %get-tuple-element.307, f32[768,256]{0,1:T(8,128)} %get-tuple-element.306, f32[]{:T(128)} %get-tuple-element.308, f32[]{:T(128)} %get-tuple-element.305), kind=kOutput, calls=%fused_computation.4.clone.1 | convolution fusion | flops 1813118976 | bytes 5505032 | tf_op jit(solution)/shard_map/while/body/eval_jaxpr/while/body/dot_general | solution.py:18
  113.3 2.9 fusion.34
  133.7 27.0 %while.26 = (s32[]{:T(128)}, f32[768,256]{0,1:T(8,128)S(1)}, s32[]{:T(128)}, f32[]{:T(128)}, f32[768,256]{0,1:T(8,128)}, /*index=5*/f32[768,768]{1,0:T(8,128)S(1)}, f32[]{:T(128)}, f32[768,256]{0,1:T(8,128)}, s32[]{:T(128)}) while((s32[]{:T(128)}, f32[768,256]{0,1:T(8,128)S(1)}, s32[]{:T(128)}, f32[]{:T(128)}, f32[768,256]{0,1:T(8,128)}, ...), condition=%wide.region_3.3_spmd, body=%wide.region_2.2_spmd.sunk | while | flops 1813118976 | bytes 7077989 | solution.py:23
  134.4 3.7 %fusion.38 = f32[768,256]{0,1:T(8,128)S(1)} fusion(f32[768,256]{0,1:T(8,128)S(1)} %copy.52, f32[768,256]{0,1:T(8,128)} %get-tuple-element.309, f32[768,768]{1,0:T(8,128)S(1)} %get-tuple-element.307, f32[768,256]{0,1:T(8,128)} %get-tuple-element.306, f32[]{:T(128)} %get-tuple-element.308, f32[]{:T(128)} %get-tuple-element.305), kind=kOutput, calls=%fused_computation.4.clone.1 | convolution fusion | flops 1813118976 | bytes 5505032 | tf_op jit(solution)/shard_map/while/body/eval_jaxpr/while/body/dot_general | solution.py:18
  138.8 3.7 %fusion.38 = f32[768,256]{0,1:T(8,128)S(1)} fusion(f32[768,256]{0,1:T(8,128)S(1)} %copy.52, f32[768,256]{0,1:T(8,128)} %get-tuple-element.309, f32[768,768]{1,0:T(8,128)S(1)} %get-tuple-element.307, f32[768,256]{0,1:T(8,128)} %get-tuple-element.306, f32[]{:T(128)} %get-tuple-element.308, f32[]{:T(128)} %get-tuple-element.305), kind=kOutput, calls=%fused_computation.4.clone.1 | convolution fusion | flops 1813118976 | bytes 5505032 | tf_op jit(solution)/shard_map/while/body/eval_jaxpr/while/body/dot_general | solution.py:18
  143.2 3.7 %fusion.38 = f32[768,256]{0,1:T(8,128)S(1)} fusion(f32[768,256]{0,1:T(8,128)S(1)} %copy.52, f32[768,256]{0,1:T(8,128)} %get-tuple-element.309, f32[768,768]{1,0:T(8,128)S(1)} %get-tuple-element.307, f32[768,256]{0,1:T(8,128)} %get-tuple-element.306, f32[]{:T(128)} %get-tuple-element.308, f32[]{:T(128)} %get-tuple-element.305), kind=kOutput, calls=%fused_computation.4.clone.1 | convolution fusion | flops 1813118976 | bytes 5505032 | tf_op jit(solution)/shard_map/while/body/eval_jaxpr/while/body/dot_general | solution.py:18
  147.6 3.7 %fusion.38 = f32[768,256]{0,1:T(8,128)S(1)} fusion(f32[768,256]{0,1:T(8,128)S(1)} %copy.52, f32[768,256]{0,1:T(8,128)} %get-tuple-element.309, f32[768,768]{1,0:T(8,128)S(1)} %get-tuple-element.307, f32[768,256]{0,1:T(8,128)} %get-tuple-element.306, f32[]{:T(128)} %get-tuple-element.308, f32[]{:T(128)} %get-tuple-element.305), kind=kOutput, calls=%fused_computation.4.clone.1 | convolution fusion | flops 1813118976 | bytes 5505032 | tf_op jit(solution)/shard_map/while/body/eval_jaxpr/while/body/dot_general | solution.py:18
  152.0 3.7 %fusion.38 = f32[768,256]{0,1:T(8,128)S(1)} fusion(f32[768,256]{0,1:T(8,128)S(1)} %copy.52, f32[768,256]{0,1:T(8,128)} %get-tuple-element.309, f32[768,768]{1,0:T(8,128)S(1)} %get-tuple-element.307, f32[768,256]{0,1:T(8,128)} %get-tuple-element.306, f32[]{:T(128)} %get-tuple-element.308, f32[]{:T(128)} %get-tuple-element.305), kind=kOutput, calls=%fused_computation.4.clone.1 | convolution fusion | flops 1813118976 | bytes 5505032 | tf_op jit(solution)/shard_map/while/body/eval_jaxpr/while/body/dot_general | solution.py:18
  156.4 3.7 %fusion.38 = f32[768,256]{0,1:T(8,128)S(1)} fusion(f32[768,256]{0,1:T(8,128)S(1)} %copy.52, f32[768,256]{0,1:T(8,128)} %get-tuple-element.309, f32[768,768]{1,0:T(8,128)S(1)} %get-tuple-element.307, f32[768,256]{0,1:T(8,128)} %get-tuple-element.306, f32[]{:T(128)} %get-tuple-element.308, f32[]{:T(128)} %get-tuple-element.305), kind=kOutput, calls=%fused_computation.4.clone.1 | convolution fusion | flops 1813118976 | bytes 5505032 | tf_op jit(solution)/shard_map/while/body/eval_jaxpr/while/body/dot_general | solution.py:18
  181.0 13.8 %while.26 = (s32[]{:T(128)}, f32[768,256]{0,1:T(8,128)S(1)}, s32[]{:T(128)}, f32[]{:T(128)}, f32[768,256]{0,1:T(8,128)}, /*index=5*/f32[768,768]{1,0:T(8,128)S(1)}, f32[]{:T(128)}, f32[768,256]{0,1:T(8,128)}, s32[]{:T(128)}) while((s32[]{:T(128)}, f32[768,256]{0,1:T(8,128)S(1)}, s32[]{:T(128)}, f32[]{:T(128)}, f32[768,256]{0,1:T(8,128)}, ...), condition=%wide.region_3.3_spmd, body=%wide.region_2.2_spmd.sunk | while | flops 1813118976 | bytes 7077989 | solution.py:23
  181.7 3.7 %fusion.38 = f32[768,256]{0,1:T(8,128)S(1)} fusion(f32[768,256]{0,1:T(8,128)S(1)} %copy.52, f32[768,256]{0,1:T(8,128)} %get-tuple-element.309, f32[768,768]{1,0:T(8,128)S(1)} %get-tuple-element.307, f32[768,256]{0,1:T(8,128)} %get-tuple-element.306, f32[]{:T(128)} %get-tuple-element.308, f32[]{:T(128)} %get-tuple-element.305), kind=kOutput, calls=%fused_computation.4.clone.1 | convolution fusion | flops 1813118976 | bytes 5505032 | tf_op jit(solution)/shard_map/while/body/eval_jaxpr/while/body/dot_general | solution.py:18
  186.1 3.7 %fusion.38 = f32[768,256]{0,1:T(8,128)S(1)} fusion(f32[768,256]{0,1:T(8,128)S(1)} %copy.52, f32[768,256]{0,1:T(8,128)} %get-tuple-element.309, f32[768,768]{1,0:T(8,128)S(1)} %get-tuple-element.307, f32[768,256]{0,1:T(8,128)} %get-tuple-element.306, f32[]{:T(128)} %get-tuple-element.308, f32[]{:T(128)} %get-tuple-element.305), kind=kOutput, calls=%fused_computation.4.clone.1 | convolution fusion | flops 1813118976 | bytes 5505032 | tf_op jit(solution)/shard_map/while/body/eval_jaxpr/while/body/dot_general | solution.py:18
  190.5 3.7 %fusion.38 = f32[768,256]{0,1:T(8,128)S(1)} fusion(f32[768,256]{0,1:T(8,128)S(1)} %copy.52, f32[768,256]{0,1:T(8,128)} %get-tuple-element.309, f32[768,768]{1,0:T(8,128)S(1)} %get-tuple-element.307, f32[768,256]{0,1:T(8,128)} %get-tuple-element.306, f32[]{:T(128)} %get-tuple-element.308, f32[]{:T(128)} %get-tuple-element.305), kind=kOutput, calls=%fused_computation.4.clone.1 | convolution fusion | flops 1813118976 | bytes 5505032 | tf_op jit(solution)/shard_map/while/body/eval_jaxpr/while/body/dot_general | solution.py:18
  215.2 13.8 %while.26 = (s32[]{:T(128)}, f32[768,256]{0,1:T(8,128)S(1)}, s32[]{:T(128)}, f32[]{:T(128)}, f32[768,256]{0,1:T(8,128)}, /*index=5*/f32[768,768]{1,0:T(8,128)S(1)}, f32[]{:T(128)}, f32[768,256]{0,1:T(8,128)}, s32[]{:T(128)}) while((s32[]{:T(128)}, f32[768,256]{0,1:T(8,128)S(1)}, s32[]{:T(128)}, f32[]{:T(128)}, f32[768,256]{0,1:T(8,128)}, ...), condition=%wide.region_3.3_spmd, body=%wide.region_2.2_spmd.sunk | while | flops 1813118976 | bytes 7077989 | solution.py:23
  215.9 3.7 %fusion.38 = f32[768,256]{0,1:T(8,128)S(1)} fusion(f32[768,256]{0,1:T(8,128)S(1)} %copy.52, f32[768,256]{0,1:T(8,128)} %get-tuple-element.309, f32[768,768]{1,0:T(8,128)S(1)} %get-tuple-element.307, f32[768,256]{0,1:T(8,128)} %get-tuple-element.306, f32[]{:T(128)} %get-tuple-element.308, f32[]{:T(128)} %get-tuple-element.305), kind=kOutput, calls=%fused_computation.4.clone.1 | convolution fusion | flops 1813118976 | bytes 5505032 | tf_op jit(solution)/shard_map/while/body/eval_jaxpr/while/body/dot_general | solution.py:18
  220.3 3.7 %fusion.38 = f32[768,256]{0,1:T(8,128)S(1)} fusion(f32[768,256]{0,1:T(8,128)S(1)} %copy.52, f32[768,256]{0,1:T(8,128)} %get-tuple-element.309, f32[768,768]{1,0:T(8,128)S(1)} %get-tuple-element.307, f32[768,256]{0,1:T(8,128)} %get-tuple-element.306, f32[]{:T(128)} %get-tuple-element.308, f32[]{:T(128)} %get-tuple-element.305), kind=kOutput, calls=%fused_computation.4.clone.1 | convolution fusion | flops 1813118976 | bytes 5505032 | tf_op jit(solution)/shard_map/while/body/eval_jaxpr/while/body/dot_general | solution.py:18
  224.7 3.7 %fusion.38 = f32[768,256]{0,1:T(8,128)S(1)} fusion(f32[768,256]{0,1:T(8,128)S(1)} %copy.52, f32[768,256]{0,1:T(8,128)} %get-tuple-element.309, f32[768,768]{1,0:T(8,128)S(1)} %get-tuple-element.307, f32[768,256]{0,1:T(8,128)} %get-tuple-element.306, f32[]{:T(128)} %get-tuple-element.308, f32[]{:T(128)} %get-tuple-element.305), kind=kOutput, calls=%fused_computation.4.clone.1 | convolution fusion | flops 1813118976 | bytes 5505032 | tf_op jit(solution)/shard_map/while/body/eval_jaxpr/while/body/dot_general | solution.py:18
  229.0 2.9 fusion.34
  237.7 8.3 %psum.14 = f32[2]{0:T(128)S(1)} all-reduce(f32[2]{0:T(128)S(1)} %compare_select_fusion), channel_id=1, replica_groups=mesh['expert'=8,'token'=4] {'token'}, use_global_device_ids=true, to_apply=%region_8.9 | all-reduce | flops 2 | bytes 16 | tf_op jit(solution)/shard_map/psum | solution.py:75
  246.1 58.1 %psum.15 = f32[]{:T(128)} all-reduce(f32[]{:T(128)} %reduce_sum.47), channel_id=1, replica_groups=mesh['expert'=8,'token'=4] {'expert','token'}, use_global_device_ids=true, to_apply=%region_10.11 | all-reduce | flops 1 | bytes 8 | tf_op jit(solution)/shard_map/psum | solution.py:76
  (105 shorter events, 83.0 us)
Async XLA Ops:
  0.6 2.7 copy-start.1
  4.3 22.7 %collective-permute-start = (bf16[2,256,768]{2,1,0:T(8,128)(2,1)S(1)}, bf16[2,256,768]{2,1,0:T(8,128)(2,1)S(1)}, u32[]{:S(2)}, u32[]{:S(2)}) collective-permute-start(bf16[2,256,768]{2,1,0:T(8,128)(2,1)S(1)} %get-tuple-element.151), channel_id=1, source_target_pairs={{0,1},{1,2},{2,3},{3,0},{4,5},{5,6},{6,7},{7,4},{8,9},{9,10},{10,1... | collective-permute-start | bytes 2359304 | tf_op jit(solution)/shard_map/ppermute | solution.py:50
  27.0 20.5 %collective-permute-start.1 = (bf16[2,256,768]{2,1,0:T(8,128)(2,1)S(1)}, bf16[2,256,768]{2,1,0:T(8,128)(2,1)S(1)}, u32[]{:S(2)}, u32[]{:S(2)}) collective-permute-start(bf16[2,256,768]{2,1,0:T(8,128)(2,1)S(1)} %collective-permute-done), channel_id=1, source_target_pairs={{0,1},{1,2},{2,3},{3,0},{4,5},{5,6},{6,7},{7,4},{8,9},{9,10},{10,1... | collective-permute-start | bytes 2359304 | tf_op jit(solution)/shard_map/ppermute | solution.py:50
  47.5 19.6 %collective-permute-start.2 = (bf16[2,256,768]{2,1,0:T(8,128)(2,1)S(1)}, bf16[2,256,768]{2,1,0:T(8,128)(2,1)S(1)}, u32[]{:S(2)}, u32[]{:S(2)}) collective-permute-start(bf16[2,256,768]{2,1,0:T(8,128)(2,1)S(1)} %collective-permute-done.1), channel_id=1, source_target_pairs={{0,1},{1,2},{2,3},{3,0},{4,5},{5,6},{6,7},{7,4},{8,9},{9,10},{10,1... | collective-permute-start | bytes 2359304 | tf_op jit(solution)/shard_map/ppermute | solution.py:50
  49.5 23.4 %copy-start.2 = (s32[4]{0:T(128)S(1)}, s32[4]{0:T(128)}, u32[]{:S(2)}) copy-start(s32[4]{0:T(128)} %param.14) | copy-start | bytes 52
  49.5 23.4 %copy-start.3 = (f32[4]{0:T(128)S(1)}, f32[4]{0:T(128)}, u32[]{:S(2)}) copy-start(f32[4]{0:T(128)} %param.15) | copy-start | bytes 52
  83.3 0.9 copy-start
  130.6 0.9 copy-start
  178.0 0.9 copy-start
  212.1 0.9 copy-start
